TPU v7x, 512 devices: a whole 4x4x16 slice. The times are simulated.
512 devices in a mesh: seq: 4 (over z_lo), fsdp: 32 (over z_hi, y, core), dp: 4 (over x).
Axes of the slice: x: 4, y: 4, z: 16 (z_hi: 4, z_lo: 4; z = z_hi * 4 + z_lo), core: 2. Of those that a mesh axis runs over, the one named last changes fastest.
Arguments:
- query: bfloat16 [128, 768, 1024], P(('fsdp', 'dp'), 'seq'), may hold values from -6 to 6
- key: bfloat16 [128, 768, 1024], P(('fsdp', 'dp'), 'seq'), may hold values from -6 to 6
- value: bfloat16 [128, 768, 1024], P(('fsdp', 'dp'), 'seq'), may hold values from -4 to 4
- out_weight: bfloat16 [1024, 2048], P('fsdp'), may hold values from -0.1875 to 0.1875
- out_grad: bfloat16 [128, 768, 2048], P(('fsdp', 'dp'), 'seq'), may hold values from -5 to 5
- block_ids: int32 [8], P('seq'), may hold values from 0 to 7, as said below
Outputs:
- query_grad: bfloat16 [128, 768, 1024], P(('fsdp', 'dp'), 'seq')
- key_grad: bfloat16 [128, 768, 1024], P(('fsdp', 'dp'), 'seq')
- value_grad: bfloat16 [128, 768, 1024], P(('fsdp', 'dp'), 'seq')
- weight_grad: bfloat16 [1024, 2048], P('fsdp')
Inputs may be any that keep to these rules, and one draw needn't show every extreme that they name: `block_ids`: each number 0 to 7 appears once, and entries 2 i and 2 i + 1 always sum to 7.
All inputs are finite; a program needn't handle non-finite values.
Results may differ from a plain program's by a relative error of at most 0.027.
Values may be sent and summed in bfloat16 or wider, within the bound.
No kernel may reach another device: no remote copies, remote signals or barrier semaphores. Data moves between devices by JAX's collectives and lax.ppermute only.
A program may use at most 64 MiB of HBM per device.

v0:
```python
import math
import jax
import jax.numpy as jnp
from jax import lax
from jax.sharding import PartitionSpec as P

HEADS = 8
HD = 128


def positions_of(block_list, block_rows):
    offsets = jnp.arange(block_rows, dtype=jnp.int32)
    return (block_list[:, None] * block_rows + offsets[None, :]).reshape(-1)


def shards(query, key, value, out_weight, out_grad, block_ids):
    tokens_here = query.shape[1]
    width_heads = query.shape[2]
    block_rows = tokens_here // block_ids.shape[0]
    score_scale = 1.0 / math.sqrt(HD)
    all_blocks = lax.all_gather(block_ids, "seq", axis=0, tiled=True)
    query_pos = positions_of(block_ids, block_rows)
    every_pos = positions_of(all_blocks, block_rows)
    key_all, value_all = (
        lax.all_gather(key, "seq", axis=1, tiled=True),
        lax.all_gather(value, "seq", axis=1, tiled=True),
    )
    query_heads = query[0].reshape(tokens_here, HEADS, HD)
    key_heads = key_all[0].reshape(-1, HEADS, HD)
    value_heads = value_all[0].reshape(-1, HEADS, HD)
    scores = (
        jnp.einsum("thd,khd->htk", query_heads, key_heads, preferred_element_type=jnp.float32)
        * score_scale
    )
    allowed = every_pos[None, :] <= query_pos[:, None]
    scores = jnp.where(allowed[None], scores, -jnp.inf)
    row_top = jnp.max(scores, axis=2, keepdims=True)
    row_total = jnp.sum(jnp.exp(scores - row_top), axis=2, keepdims=True)
    log_total = row_top + jnp.log(row_total)
    weights = jnp.exp(scores - log_total)
    weights_low = weights.astype(jnp.bfloat16)
    attended = jnp.einsum(
        "htk,khd->thd", weights_low, value_heads, preferred_element_type=jnp.float32
    ).astype(jnp.bfloat16)
    grad_rows = out_grad[0]
    attn_grad = lax.dot_general(
        grad_rows,
        lax.all_gather(out_weight, "fsdp", axis=0, tiled=True),
        (((1,), (1,)), ((), ())),
        preferred_element_type=jnp.float32,
    ).astype(jnp.bfloat16)
    attended_flat = attended.reshape(tokens_here, width_heads)
    weight_shard = lax.psum_scatter(
        lax.dot_general(
            attended_flat, grad_rows, (((0,), (0,)), ((), ())), preferred_element_type=jnp.float32
        ).astype(jnp.bfloat16),
        "fsdp",
        scatter_dimension=0,
        tiled=True,
    ).astype(jnp.float32)
    token_count = tokens_here * lax.axis_size("seq") * lax.axis_size("fsdp") * lax.axis_size("dp")
    weight_grad = (lax.psum(weight_shard, ("seq", "dp")) * (1.0 / math.sqrt(token_count))).astype(
        jnp.bfloat16
    )
    grad_heads = attn_grad.reshape(tokens_here, HEADS, HD)
    row_delta = jnp.einsum("thd,thd->ht", grad_heads, attended, preferred_element_type=jnp.float32)
    prob_grad = jnp.einsum(
        "thd,khd->htk", grad_heads, value_heads, preferred_element_type=jnp.float32
    )
    score_grad = (weights * (prob_grad - row_delta[:, :, None])).astype(jnp.bfloat16)
    query_grad = (
        jnp.einsum("htk,khd->thd", score_grad, key_heads, preferred_element_type=jnp.float32)
        * score_scale
    ).astype(jnp.bfloat16)
    query_all, grad_all = (
        lax.all_gather(query, "seq", axis=1, tiled=True),
        lax.all_gather(attn_grad[None], "seq", axis=1, tiled=True),
    )
    totals_all, deltas_all = (
        lax.all_gather(log_total[:, :, 0][None], "seq", axis=2, tiled=True),
        lax.all_gather(row_delta[None], "seq", axis=2, tiled=True),
    )
    local_keys = key[0].reshape(tokens_here, HEADS, HD)
    local_values = value[0].reshape(tokens_here, HEADS, HD)
    gathered_queries = query_all[0].reshape(-1, HEADS, HD)
    gathered_grads = grad_all[0].reshape(-1, HEADS, HD)
    back_scores = (
        jnp.einsum("khd,qhd->hkq", local_keys, gathered_queries, preferred_element_type=jnp.float32)
        * score_scale
    )
    back_allowed = query_pos[:, None] <= every_pos[None, :]
    back_scores = jnp.where(back_allowed[None], back_scores, -jnp.inf)
    back_weights = jnp.exp(back_scores - totals_all[0][:, None, :])
    back_low = back_weights.astype(jnp.bfloat16)
    back_prob_grad = jnp.einsum(
        "qhd,khd->hkq", gathered_grads, local_values, preferred_element_type=jnp.float32
    )
    back_score_grad = (back_weights * (back_prob_grad - deltas_all[0][:, None, :])).astype(
        jnp.bfloat16
    )
    key_grad = (
        jnp.einsum(
            "hkq,qhd->khd", back_score_grad, gathered_queries, preferred_element_type=jnp.float32
        )
        * score_scale
    ).astype(jnp.bfloat16)
    value_grad = jnp.einsum(
        "hkq,qhd->khd", back_low, gathered_grads, preferred_element_type=jnp.float32
    ).astype(jnp.bfloat16)
    return (
        query_grad.reshape(tokens_here, width_heads)[None],
        key_grad.reshape(tokens_here, width_heads)[None],
        value_grad.reshape(tokens_here, width_heads)[None],
        weight_grad,
    )


def solution(mesh):
    in_specs = (
        P(("fsdp", "dp"), "seq", None),
        P(("fsdp", "dp"), "seq", None),
        P(("fsdp", "dp"), "seq", None),
        P("fsdp", None),
        P(("fsdp", "dp"), "seq", None),
        P("seq"),
    )
    out_specs = (
        P(("fsdp", "dp"), "seq", None),
        P(("fsdp", "dp"), "seq", None),
        P(("fsdp", "dp"), "seq", None),
        P("fsdp", None),
    )
    return jax.shard_map(shards, mesh=mesh, in_specs=in_specs, out_specs=out_specs, check_vma=False)
```

profile of v0, /device:TPU:16, one launch (start us, length us, event | category | flops | bytes accessed | tf_op | source)
XLA Modules:
  0.0 531.4 jit_solution(5790894048885190867)
XLA Ops:
  8.0 0.7 all-gather.11.cloned.1.call-update
  10.0 1.3 dynamic-slice
  12.0 0.9 dynamic-update-slice
  12.8 9.1 %all-reduce = s32[8]{0:T(128)S(1)} all-reduce(s32[8]{0:T(128)S(1)} %dynamic-update-slice), channel_id=1, replica_groups=mesh['seq'=4,'fsdp'=32,'dp'=4] {'seq'}, use_global_device_ids=true, to_apply=%add | all-reduce | flops 8 | bytes 64
  22.9 1.1 copy.64
  24.0 86.7 %all-gather.13.cloned.1.call-done = bf16[1024,2048]{1,0:T(8,128)(2,1)} async-done(((bf16[32,2048]{1,0:T(8,128)(2,1)}), bf16[1024,2048]{1,0:T(8,128)(2,1)}) %all-gather.13.cloned.1.call-update) | async-done | bytes 4194320 | tf_op jit(solution)/shard_map/all_gather | solution.py:48
  110.6 4.5 convolution_convert_fusion.1
  115.4 39.8 %all-gather.11.cloned.1.call-done = bf16[1,768,1024]{2,1,0:T(8,128)(2,1)} async-done(((bf16[1,192,1024]{2,1,0:T(8,128)(2,1)}), bf16[1,768,1024]{2,1,0:T(8,128)(2,1)}) %all-gather.11.cloned.1.call-update) | async-done | bytes 1572880 | tf_op jit(solution)/shard_map/all_gather | solution.py:25
  155.2 1.7 copy.28
  157.0 46.7 %all-gather.15.cloned.1.call-done = bf16[1,768,1024]{2,1,0:T(8,128)(2,1)} async-done(((bf16[1,192,1024]{2,1,0:T(8,128)(2,1)}), bf16[1,768,1024]{2,1,0:T(8,128)(2,1)}) %all-gather.15.cloned.1.call-update) | async-done | bytes 1572880 | tf_op jit(solution)/shard_map/all_gather | solution.py:26
  203.7 2.6 copy.31
  206.3 1.0 fusion.3
  207.3 1.2 exponential_reduce_fusion
  208.7 1.1 copy-done.3
  209.9 1.6 multiply_reduce_fusion
  211.6 3.4 convolution_convert_fusion
  215.0 0.8 copy.67
  215.9 13.1 %all-gather.3 = f32[4,192,8]{1,2,0:T(8,128)S(1)} all-gather(f32[1,192,8]{1,2,0:T(8,128)S(1)} %bitcast.115), channel_id=2, replica_groups=mesh['seq'=4,'fsdp'=32,'dp'=4] {'seq'}, dimensions={0}, use_global_device_ids=true | all-gather | bytes 30720 | tf_op jit(solution)/shard_map/all_gather | solution.py:80
  229.1 22.9 %all-gather.17.cloned.1.call-done = bf16[1,768,1024]{2,1,0:T(8,128)(2,1)} async-done(((bf16[1,192,1024]{2,1,0:T(8,128)(2,1)}), bf16[1,768,1024]{2,1,0:T(8,128)(2,1)}) %all-gather.17.cloned.1.call-update) | async-done | bytes 1572880 | tf_op jit(solution)/shard_map/all_gather | solution.py:76
  252.0 1.7 copy.37
  253.7 2.9 fusion.72
  256.7 6.3 %fusion.56 = bf16[192,8,128]{2,0,1:T(8,128)(2,1)} fusion(bf16[768,8,128]{0,2,1:T(8,128)(2,1)} %bitcast.105, f32[8,192,768]{2,1,0:T(8,128)} %copy-done.1, f32[8,192]{1,0:T(8,128)S(1)} %get-tuple-element.8, f32[8,192]{1,0:T(8,128)S(1)} %log_add_fusion, pred[192,768]{1,0:T(8,128)(4,1)S(1)} %get-tuple-element.5, bf16[768,8,128]{0,2,1:T(8,128)(2,1)} %bitcast.106, ...), kind=kOutput, calls=%fused_computation.39 | convolution fusion | flops 611450880 | bytes 8810496 | tf_op jit(solution)/shard_map/htk,khd->thd/dot_general | solution.py:72
  262.9 1.3 copy.36
  264.2 0.9 broadcast_in_dim_reshape.6
  265.1 13.4 %all-gather.4 = f32[4,192,8]{1,2,0:T(8,128)S(1)} all-gather(f32[1,192,8]{1,2,0:T(8,128)S(1)} %bitcast.119), channel_id=4, replica_groups=mesh['seq'=4,'fsdp'=32,'dp'=4] {'seq'}, dimensions={0}, use_global_device_ids=true | all-gather | bytes 30720 | tf_op jit(solution)/shard_map/all_gather | solution.py:81
  278.6 22.4 %all-gather.19.cloned.1.call-done = bf16[768,1024]{1,0:T(8,128)(2,1)} async-done(((bf16[192,1024]{1,0:T(8,128)(2,1)}), bf16[768,1024]{1,0:T(8,128)(2,1)}) %all-gather.19.cloned.1.call-update) | async-done | bytes 1572880 | tf_op jit(solution)/shard_map/all_gather | solution.py:77
  301.0 4.8 fusion.51
  306.1 0.9 broadcast_in_dim_reshape.14
  307.0 4.2 fusion.57
  311.5 0.9 broadcast_in_dim_reshape.15
  312.4 129.9 %reduce-scatter.2.cloned.1.call-done = bf16[32,2048]{1,0:T(8,128)(2,1)} async-done(((bf16[1024,2048]{1,0:T(8,128)(2,1)}), bf16[32,2048]{1,0:T(8,128)(2,1)}) %reduce-scatter.2.cloned.1.call-update) | async-done | bytes 131088 | tf_op jit(solution)/shard_map/reduce_scatter | solution.py:53
  442.3 81.5 %all-reduce.2 = f32[32,2048]{1,0:T(8,128)S(1)} all-reduce(bf16[32,2048]{1,0:T(8,128)(2,1)} %reduce-scatter.2.cloned.1.call-done), channel_id=1, replica_groups=mesh['seq'=4,'fsdp'=32,'dp'=4] {'seq','dp'}, use_global_device_ids=true, to_apply=%region_3.4 | all-reduce | flops 65536 | bytes 393216 | tf_op jit(solution)/shard_map/psum | solution.py:62
  (45 shorter events, 5.0 us)
Async XLA Ops:
  7.2 103.5 %copy-start = (bf16[1,192,2048]{2,1,0:T(8,128)(2,1)S(1)}, bf16[1,192,2048]{2,1,0:T(8,128)(2,1)}, u32[]{:S(2)}) copy-start(bf16[1,192,2048]{2,1,0:T(8,128)(2,1)} %param.10) | copy-start | bytes 2359300
  7.2 103.5 %all-gather.13.cloned.1.call-start = ((), (), s32[]{:S(2)}) async-start(), calls=%async_computation.2 | async-start | bytes 4325376 | tf_op jit(solution)/shard_map/all_gather | solution.py:48
  7.9 147.3 %all-gather.11.cloned.1.call-start = ((), (), s32[]{:S(2)}) async-start(), calls=%async_computation.1 | async-start | bytes 1966080 | tf_op jit(solution)/shard_map/all_gather | solution.py:25
  8.7 195.0 %all-gather.15.cloned.1.call-start = ((), (), s32[]{:S(2)}) async-start(), calls=%async_computation.3 | async-start | bytes 1966080 | tf_op jit(solution)/shard_map/all_gather | solution.py:26
  9.4 242.6 %all-gather.17.cloned.1.call-start = ((), (), s32[]{:S(2)}) async-start(), calls=%async_computation.4 | async-start | bytes 1966080 | tf_op jit(solution)/shard_map/all_gather | solution.py:76
  10.0 291.0 %all-gather.19.cloned.1.call-start = ((), (), s32[]{:S(2)}) async-start(), calls=%async_computation.6 | async-start | bytes 1966080 | tf_op jit(solution)/shard_map/all_gather | solution.py:77
  115.1 327.2 %reduce-scatter.2.cloned.1.call-start = ((), (), s32[]{:S(2)}) async-start(), calls=%async_computation.5 | async-start | bytes 4325376 | tf_op jit(solution)/shard_map/reduce_scatter | solution.py:53
  156.9 50.3 %copy-start.2 = (bf16[1,768,1024]{1,2,0:T(8,128)(2,1)}, bf16[1,768,1024]{1,2,0:T(8,128)(2,1)S(1)}, u32[]{:S(2)}) copy-start(bf16[1,768,1024]{1,2,0:T(8,128)(2,1)S(1)} %copy.28) | copy-start | bytes 4718596
  206.3 2.3 copy-start.6
  207.3 4.2 copy-start.1
  207.3 2.6 copy-start.3
  211.5 3.4 copy-start.4
  211.5 3.5 copy-start.5
  256.7 44.3 %copy-start.7 = (bf16[24,8,8,128]{3,2,1,0:T(8,128)(2,1)S(1)}, bf16[24,8,8,128]{3,2,1,0:T(8,128)(2,1)}, u32[]{:S(2)}) copy-start(bf16[24,8,8,128]{3,2,1,0:T(8,128)(2,1)} %copy.67) | copy-start | bytes 1179652
Sparse Core Ops, SparseCore 0:
  11.1 99.4 all-gather.12
  112.7 42.4 all-gather.10
  157.3 46.2 all-gather.14
  205.6 46.3 all-gather.16
  254.5 46.4 all-gather.18
  305.4 136.9 reduce-scatter.1
where the time goes:
time: 532 us; the launch traced here: 531 us
  waiting for transfers between devices  351 us (66%)
  blocking collectives  117 us (22%)
  matrix products  28.8 us (5%)
  local copies, waits for them, and re-layouts  16.2 us (3%)
  between operations  15 us (3%)
    reduce_scatter x1, waiting for transfers between devices, shards(): lax.psum_scatter(lax.dot_general(attended_flat, grad_rows, (((0,), (0,)),...  130 us
    all_gather x1, waiting for transfers between devices, shards(): lax.all_gather(out_weight, 'fsdp', axis=0, tiled=True)  86.7 us
    psum x1, blocking collectives, shards(): lax.psum(weight_shard, ('seq', 'dp')) * (1.0 / math.sqrt(token_count))  81.5 us
    all_gather x1, waiting for transfers between devices, shards(): lax.all_gather(value, 'seq', axis=1, tiled=True)  46.7 us
    all_gather x1, waiting for transfers between devices, shards(): lax.all_gather(key, 'seq', axis=1, tiled=True)  39.8 us
    all_gather x1, waiting for transfers between devices, shards(): lax.all_gather(query, 'seq', axis=1, tiled=True)  22.9 us
    all_gather x1, waiting for transfers between devices, shards(): lax.all_gather(attn_grad[None], 'seq', axis=1, tiled=True)  22.4 us
    all_gather x1, blocking collectives, shards(): lax.all_gather(row_delta[None], 'seq', axis=2, tiled=True)  13.4 us
  transfers between devices with their start and end apart: 6, of which 6 were waited for; matrix products, arithmetic and copies ran while one was open for 9% of the time, Pallas kernels for 0%

commit v1 on v0

--- a/solution.py
+++ b/solution.py
@@ -59,9 +59,10 @@
         tiled=True,
     ).astype(jnp.float32)
     token_count = tokens_here * lax.axis_size("seq") * lax.axis_size("fsdp") * lax.axis_size("dp")
-    weight_grad = (lax.psum(weight_shard, ("seq", "dp")) * (1.0 / math.sqrt(token_count))).astype(
-        jnp.bfloat16
-    )
+    weight_grad = (
+        jnp.sum(lax.all_gather(weight_shard, ("seq", "dp")), axis=0)
+        * (1.0 / math.sqrt(token_count))
+    ).astype(jnp.bfloat16)
     grad_heads = attn_grad.reshape(tokens_here, HEADS, HD)
     row_delta = jnp.einsum("thd,thd->ht", grad_heads, attended, preferred_element_type=jnp.float32)
     prob_grad = jnp.einsum(

time: 532 us -> 551 us (1.036)
  the two profiles are of different devices: /device:TPU:16 before, /device:TPU:2 now
where the time goes in v1:
time: 551 us
  waiting for transfers between devices  445 us (81%)
  blocking collectives  35.6 us (6%)
  matrix products  30.1 us (5%)
  local copies, waits for them, and re-layouts  17.1 us (3%)
  between operations  15 us (3%)
  other arithmetic  7.08 us (1%)
    reduce_scatter x1, waiting for transfers between devices, shards(): lax.psum_scatter(lax.dot_general(attended_flat, grad_rows, (((0,), (0,)),...  133 us
    all_gather x1, waiting for transfers between devices, shards(): lax.all_gather(out_weight, 'fsdp', axis=0, tiled=True)  90.8 us
    all_gather x1, waiting for transfers between devices, shards(): lax.all_gather(weight_shard, ('seq', 'dp'))  83.5 us
    all_gather x1, waiting for transfers between devices, shards(): lax.all_gather(value, 'seq', axis=1, tiled=True)  46.7 us
    all_gather x1, waiting for transfers between devices, shards(): lax.all_gather(key, 'seq', axis=1, tiled=True)  37.8 us
    all_gather x1, waiting for transfers between devices, shards(): lax.all_gather(query, 'seq', axis=1, tiled=True)  27.5 us
    all_gather x1, waiting for transfers between devices, shards(): lax.all_gather(attn_grad[None], 'seq', axis=1, tiled=True)  22.6 us
    all_gather x1, blocking collectives, shards(): lax.all_gather(row_delta[None], 'seq', axis=2, tiled=True)  13.4 us
  transfers between devices with their start and end apart: 7, of which 7 were waited for; matrix products, arithmetic and copies ran while one was open for 7% of the time, Pallas kernels for 0%

profile of v1, /device:TPU:2, one launch (start us, length us, event | category | flops | bytes accessed | tf_op | source)
XLA Modules:
  0.0 550.5 jit_solution(11012804662886660687)
XLA Ops:
  9.4 1.3 dynamic-slice
  11.4 0.9 dynamic-update-slice
  12.2 9.1 %all-reduce = s32[8]{0:T(128)S(1)} all-reduce(s32[8]{0:T(128)S(1)} %dynamic-update-slice), channel_id=1, replica_groups=mesh['seq'=4,'fsdp'=32,'dp'=4] {'seq'}, use_global_device_ids=true, to_apply=%add | all-reduce | flops 8 | bytes 64
  22.3 1.1 copy.64
  23.6 37.8 %all-gather.13.cloned.1.call-done = bf16[1,768,1024]{2,1,0:T(8,128)(2,1)} async-done(((bf16[1,192,1024]{2,1,0:T(8,128)(2,1)}), bf16[1,768,1024]{2,1,0:T(8,128)(2,1)}) %all-gather.13.cloned.1.call-update) | async-done | bytes 1572880 | tf_op jit(solution)/shard_map/all_gather | solution.py:25
  61.4 1.7 copy.28
  63.1 46.7 %all-gather.17.cloned.1.call-done = bf16[1,768,1024]{2,1,0:T(8,128)(2,1)} async-done(((bf16[1,192,1024]{2,1,0:T(8,128)(2,1)}), bf16[1,768,1024]{2,1,0:T(8,128)(2,1)}) %all-gather.17.cloned.1.call-update) | async-done | bytes 1572880 | tf_op jit(solution)/shard_map/all_gather | solution.py:26
  109.8 2.6 copy.31
  112.4 1.0 fusion.3
  113.5 2.1 copy-done.1
  115.6 1.2 exponential_reduce_fusion
  116.8 90.8 %all-gather.15.cloned.1.call-done = bf16[1024,2048]{1,0:T(8,128)(2,1)} async-done(((bf16[32,2048]{1,0:T(8,128)(2,1)}), bf16[1024,2048]{1,0:T(8,128)(2,1)}) %all-gather.15.cloned.1.call-update) | async-done | bytes 4194320 | tf_op jit(solution)/shard_map/all_gather | solution.py:48
  207.6 3.7 convolution_convert_fusion.1
  211.5 3.9 multiply_reduce_fusion
  215.4 3.3 convolution_convert_fusion
  219.9 133.3 %reduce-scatter.2.cloned.1.call-done = bf16[32,2048]{1,0:T(8,128)(2,1)} async-done(((bf16[1024,2048]{1,0:T(8,128)(2,1)}), bf16[32,2048]{1,0:T(8,128)(2,1)}) %reduce-scatter.2.cloned.1.call-update) | async-done | bytes 131088 | tf_op jit(solution)/shard_map/reduce_scatter | solution.py:53
  353.2 1.6 all_gather.44
  355.8 13.1 %all-gather.4 = f32[4,192,8]{1,2,0:T(8,128)S(1)} all-gather(f32[1,192,8]{1,2,0:T(8,128)S(1)} %bitcast.117), channel_id=2, replica_groups=mesh['seq'=4,'fsdp'=32,'dp'=4] {'seq'}, dimensions={0}, use_global_device_ids=true | all-gather | bytes 30720 | tf_op jit(solution)/shard_map/all_gather | solution.py:81
  369.0 27.5 %all-gather.19.cloned.1.call-done = bf16[1,768,1024]{2,1,0:T(8,128)(2,1)} async-done(((bf16[1,192,1024]{2,1,0:T(8,128)(2,1)}), bf16[1,768,1024]{2,1,0:T(8,128)(2,1)}) %all-gather.19.cloned.1.call-update) | async-done | bytes 1572880 | tf_op jit(solution)/shard_map/all_gather | solution.py:77
  396.5 1.7 copy.37
  398.2 2.9 fusion.72
  401.1 6.3 %fusion.56 = bf16[192,8,128]{2,0,1:T(8,128)(2,1)} fusion(bf16[768,8,128]{0,2,1:T(8,128)(2,1)} %bitcast.106, f32[8,192,768]{2,1,0:T(8,128)} %copy-done.1, f32[8,192]{1,0:T(8,128)S(1)} %get-tuple-element.8, f32[8,192]{1,0:T(8,128)S(1)} %log_add_fusion, pred[192,768]{1,0:T(8,128)(4,1)S(1)} %get-tuple-element.5, bf16[768,8,128]{0,2,1:T(8,128)(2,1)} %bitcast.108, ...), kind=kOutput, calls=%fused_computation.39 | convolution fusion | flops 611450880 | bytes 8810496 | tf_op jit(solution)/shard_map/htk,khd->thd/dot_general | solution.py:73
  407.4 1.3 copy.36
  408.7 0.9 broadcast_in_dim_reshape.6
  409.6 13.4 %all-gather.5 = f32[4,192,8]{1,2,0:T(8,128)S(1)} all-gather(f32[1,192,8]{1,2,0:T(8,128)S(1)} %bitcast.121), channel_id=4, replica_groups=mesh['seq'=4,'fsdp'=32,'dp'=4] {'seq'}, dimensions={0}, use_global_device_ids=true | all-gather | bytes 30720 | tf_op jit(solution)/shard_map/all_gather | solution.py:82
  423.1 22.6 %all-gather.21.cloned.1.call-done = bf16[768,1024]{1,0:T(8,128)(2,1)} async-done(((bf16[192,1024]{1,0:T(8,128)(2,1)}), bf16[768,1024]{1,0:T(8,128)(2,1)}) %all-gather.21.cloned.1.call-update) | async-done | bytes 1572880 | tf_op jit(solution)/shard_map/all_gather | solution.py:78
  445.7 4.8 fusion.51
  450.8 0.9 broadcast_in_dim_reshape.14
  451.7 4.2 fusion.57
  456.2 0.9 broadcast_in_dim_reshape.15
  457.1 83.5 %all-gather.23.cloned.1.call-done = f32[512,2048]{1,0:T(8,128)} async-done(((f32[32,2048]{1,0:T(8,128)}), f32[512,2048]{1,0:T(8,128)}) %all-gather.23.cloned.1.call-update) | async-done | bytes 4194320 | tf_op jit(solution)/shard_map/all_gather | solution.py:63
  540.6 2.4 reduce_sum.19
  (51 shorter events, 7.1 us)
Async XLA Ops:
  7.2 200.5 %copy-start = (bf16[1,192,2048]{2,1,0:T(8,128)(2,1)S(1)}, bf16[1,192,2048]{2,1,0:T(8,128)(2,1)}, u32[]{:S(2)}) copy-start(bf16[1,192,2048]{2,1,0:T(8,128)(2,1)} %param.10) | copy-start | bytes 2359300
  7.2 54.2 %all-gather.13.cloned.1.call-start = ((), (), s32[]{:S(2)}) async-start(), calls=%async_computation.1 | async-start | bytes 1966080 | tf_op jit(solution)/shard_map/all_gather | solution.py:25
  7.9 101.9 %all-gather.17.cloned.1.call-start = ((), (), s32[]{:S(2)}) async-start(), calls=%async_computation.3 | async-start | bytes 1966080 | tf_op jit(solution)/shard_map/all_gather | solution.py:26
  8.7 199.0 %all-gather.15.cloned.1.call-start = ((), (), s32[]{:S(2)}) async-start(), calls=%async_computation.2 | async-start | bytes 4325376 | tf_op jit(solution)/shard_map/all_gather | solution.py:48
  9.4 343.9 %reduce-scatter.2.cloned.1.call-start = ((), (), s32[]{:S(2)}) async-start(), calls=%async_computation.5 | async-start | bytes 4325376 | tf_op jit(solution)/shard_map/reduce_scatter | solution.py:53
  63.1 50.3 %copy-start.2 = (bf16[1,768,1024]{1,2,0:T(8,128)(2,1)}, bf16[1,768,1024]{1,2,0:T(8,128)(2,1)S(1)}, u32[]{:S(2)}) copy-start(bf16[1,768,1024]{1,2,0:T(8,128)(2,1)S(1)} %copy.28) | copy-start | bytes 4718596
  113.5 2.1 copy-start.1
  116.8 94.7 %copy-start.3 = (bf16[1,768,1024]{1,2,0:T(8,128)(2,1)S(1)}, bf16[1,768,1024]{1,2,0:T(8,128)(2,1)}, u32[]{:S(2)}) copy-start(bf16[1,768,1024]{1,2,0:T(8,128)(2,1)} %copy.31) | copy-start | bytes 4718596
  211.4 4.1 copy-start.6
  218.7 136.2 %copy-start.4 = (bf16[1,192,1024]{2,1,0:T(8,128)(2,1)S(1)}, bf16[1,192,1024]{2,1,0:T(8,128)(2,1)}, u32[]{:S(2)}) copy-start(bf16[1,192,1024]{2,1,0:T(8,128)(2,1)} %param.7) | copy-start | bytes 1179652
  218.7 136.3 %copy-start.5 = (bf16[1,192,1024]{2,1,0:T(8,128)(2,1)S(1)}, bf16[1,192,1024]{2,1,0:T(8,128)(2,1)}, u32[]{:S(2)}) copy-start(bf16[1,192,1024]{2,1,0:T(8,128)(2,1)} %param.8) | copy-start | bytes 1179652
  218.7 177.8 %all-gather.19.cloned.1.call-start = ((), (), s32[]{:S(2)}) async-start(), calls=%async_computation.4 | async-start | bytes 1966080 | tf_op jit(solution)/shard_map/all_gather | solution.py:77
  219.3 226.3 %all-gather.21.cloned.1.call-start = ((), (), s32[]{:S(2)}) async-start(), calls=%async_computation.6 | async-start | bytes 1966080 | tf_op jit(solution)/shard_map/all_gather | solution.py:78
  219.9 320.7 %all-gather.23.cloned.1.call-start = ((), (), s32[]{:S(2)}) async-start(), calls=%async_computation.7 | async-start | bytes 4456448 | tf_op jit(solution)/shard_map/all_gather | solution.py:63
  369.0 32.1 %copy-start.7 = (bf16[192,1024]{1,0:T(8,128)(2,1)S(1)}, bf16[192,1024]{1,0:T(8,128)(2,1)}, u32[]{:S(2)}) copy-start(bf16[192,1024]{1,0:T(8,128)(2,1)} %copy-done.6) | copy-start | bytes 1179652
  401.1 44.5 %copy-start.8 = (bf16[24,8,8,128]{3,2,1,0:T(8,128)(2,1)S(1)}, bf16[24,8,8,128]{3,2,1,0:T(8,128)(2,1)}, u32[]{:S(2)}) copy-start(bf16[24,8,8,128]{3,2,1,0:T(8,128)(2,1)} %copy.67) | copy-start | bytes 1179652
Sparse Core Ops, SparseCore 0:
  10.1 51.2 all-gather.12
  63.5 46.2 all-gather.16
  113.0 94.6 all-gather.14
  218.9 134.3 reduce-scatter.1
  355.4 41.0 all-gather.18
  399.3 46.3 all-gather.20
  448.0 92.5 all-gather.22
